TPU v7x, 32 devices: a whole 2x2x4 slice. The times are simulated.
32 devices in a mesh: blk: 4 (over y, core), order: 8 (over z, x).
Axes of the slice: x: 2, y: 2, z: 4, core: 2. Of those that a mesh axis runs over, the one named last changes fastest.
Arguments:
- sky_maps: float32 [16, 64, 8192], P(None, ('blk', 'order')), may hold values from -6 to 6
- wigner_d: bfloat16 [64, 1536, 2048], P(None, 'blk', 'order'), may hold values from -0.75 to 0.75
- order_of_slot: int32 [2048], replicated, may hold values from 0 to 2047, each once
- kernel: float32 [8, 2, 1536], P(None, None, 'blk'), may hold values from -6 to 6
Outputs:
- wavelet_coef: bfloat16 [8, 16, 2, 1536, 2048], P(None, None, None, 'blk', 'order')
Inputs may be any that keep to these rules, and one draw needn't show every extreme that they name: `order_of_slot`: every order appears in exactly one slot.
All inputs are finite; a program needn't handle non-finite values.
Results may differ from a plain program's by a relative error of at most 0.0049.
Values may be sent and summed in bfloat16 or wider, within the bound.
No kernel may reach another device: no remote copies, remote signals or barrier semaphores. Data moves between devices by JAX's collectives and lax.ppermute only.
A program may use at most 192 MiB of HBM per device.

v0:
```python
import math
import jax
import jax.numpy as jnp
from jax import lax
from jax.sharding import PartitionSpec as P

DEG_LO = 512
HIGHEST = lax.Precision.HIGHEST
RADIX = 128


def cycle_spectrum(sky_maps, orders):
    maps_count = sky_maps.shape[0]
    cycle_count = sky_maps.shape[1]
    samples = sky_maps.shape[2]
    outer_len = samples // RADIX
    order_blocks = orders // RADIX
    values = sky_maps.reshape(maps_count, cycle_count, RADIX, outer_len)
    inner_idx = jnp.arange(RADIX, dtype=jnp.int32)
    outer_idx = jnp.arange(outer_len, dtype=jnp.int32)
    block_idx = jnp.arange(order_blocks, dtype=jnp.int32)
    inner_angle = (
        2.0
        * math.pi
        / RADIX
        * (inner_idx[:, None] * inner_idx[None, :] % RADIX).astype(jnp.float32)
    )
    inner_re = jnp.einsum("abkj,km->abjm", values, jnp.cos(inner_angle), precision=HIGHEST)
    inner_im = -jnp.einsum("abkj,km->abjm", values, jnp.sin(inner_angle), precision=HIGHEST)
    twist_angle = (
        2.0 * math.pi / samples * (outer_idx[:, None] * inner_idx[None, :]).astype(jnp.float32)
    )
    twist_cos = jnp.cos(twist_angle)
    twist_sin = jnp.sin(twist_angle)
    turned_re = inner_re * twist_cos + inner_im * twist_sin
    turned_im = inner_im * twist_cos - inner_re * twist_sin
    outer_angle = (
        2.0
        * math.pi
        / outer_len
        * (block_idx[:, None] * outer_idx[None, :] % outer_len).astype(jnp.float32)
    )
    outer_cos = jnp.cos(outer_angle)
    outer_sin = jnp.sin(outer_angle)
    final_re = jnp.einsum("abjm,ij->abim", turned_re, outer_cos, precision=HIGHEST) + jnp.einsum(
        "abjm,ij->abim", turned_im, outer_sin, precision=HIGHEST
    )
    final_im = jnp.einsum("abjm,ij->abim", turned_im, outer_cos, precision=HIGHEST) - jnp.einsum(
        "abjm,ij->abim", turned_re, outer_sin, precision=HIGHEST
    )
    factor = 1.0 / math.sqrt(samples)
    stacked = jnp.stack(
        [
            final_re.reshape(maps_count, cycle_count, orders),
            final_im.reshape(maps_count, cycle_count, orders),
        ],
        axis=0,
    )
    return (stacked * factor).astype(jnp.bfloat16)


def add_cycles(piece, table):
    term = jnp.einsum("mrcs,rjs->mcjs", piece, table, preferred_element_type=jnp.float32)
    return term


def local(sky_maps, wigner_d, order_of_slot, kernel):
    orders = order_of_slot.shape[0]
    deg_count = wigner_d.shape[1]
    slot_count = wigner_d.shape[2]
    maps_count = sky_maps.shape[0]
    cycle_count = sky_maps.shape[1]
    groups = lax.axis_size("order")
    cycle_groups = lax.axis_size("blk")
    spectrum = cycle_spectrum(sky_maps, orders)
    slot_table = order_of_slot.reshape(groups, slot_count)
    order_ids = jnp.arange(orders, dtype=jnp.int32)
    one_hot = (order_ids[:, None, None] == slot_table[None, :, :]).astype(jnp.bfloat16)
    by_owner = jnp.einsum(
        "cmro,ogs->mgrcs", spectrum, one_hot, preferred_element_type=jnp.float32
    ).astype(jnp.bfloat16)
    copies = jnp.broadcast_to(
        by_owner[:, None], (maps_count, cycle_groups, groups, cycle_count, 2, slot_count)
    )
    copies = copies.reshape(maps_count, cycle_groups * groups * cycle_count, 2, slot_count)
    every_cycle = lax.all_to_all(copies, ("blk", "order"), split_axis=1, concat_axis=1, tiled=True)
    harmonic = add_cycles(every_cycle, wigner_d)
    my_orders = lax.dynamic_slice_in_dim(
        order_of_slot, lax.axis_index("order") * slot_count, slot_count, 0
    )
    degree = DEG_LO + lax.axis_index("blk") * deg_count + jnp.arange(deg_count, dtype=jnp.int32)
    live = degree[:, None] >= my_orders[None, :]
    real_part = jnp.where(live[None], harmonic[:, 0], 0.0)[None, :, None]
    imag_part = jnp.where(live[None], harmonic[:, 1], 0.0)[None, :, None]
    kern_re = kernel[:, 0, :]
    kern_im = kernel[:, 1, :]
    first = jnp.stack([kern_re, -kern_im], axis=1)[:, None, :, :, None]
    second = jnp.stack([kern_im, kern_re], axis=1)[:, None, :, :, None]
    return (real_part * first + imag_part * second).astype(jnp.bfloat16)


def solution(mesh):
    return jax.shard_map(
        local,
        mesh=mesh,
        in_specs=(
            P(None, ("blk", "order"), None),
            P(None, "blk", "order"),
            P(),
            P(None, None, "blk"),
        ),
        out_specs=P(None, None, None, "blk", "order"),
        check_vma=False,
    )
```

profile of v0, /device:TPU:0, one launch (start us, length us, event | category | flops | bytes accessed | tf_op | source)
XLA Modules:
  0.0 104.0 jit_solution(6579013343517247745)
XLA Ops:
  0.0 0.1 fusion.31
  0.1 2.3 %reshape.86 = f32[16,2,128,64]{3,2,1,0:T(8,128)S(1)} reshape(f32[16,2,8192]{2,1,0:T(2,128)} %param.4) | data formatting | bytes 2097152 | tf_op jit(solution)/shard_map/reshape | solution.py:18
  2.4 0.0 copy-start
  2.5 1.3 %copy-done = f32[16,2,128,64]{3,2,1,0:T(8,128)} copy-done((f32[16,2,128,64]{3,2,1,0:T(8,128)}, f32[16,2,128,64]{3,2,1,0:T(8,128)S(1)}, u32[]{:S(2)}) %copy-start) | copy-done | bytes 1048600
  3.8 0.0 copy-start.2
  3.8 3.5 %convolution_bitcast_fusion.1 = f32[16,2,64,128]{3,2,1,0:T(8,128)S(1)} fusion(f32[16,2,128,64]{3,2,1,0:T(8,128)S(1)} %reshape.86), kind=kOutput, calls=%fused_computation.12 | convolution fusion | flops 402882560 | bytes 2097152 | tf_op jit(solution)/shard_map/abkj,km->abjm/dot_general | solution.py:28
  7.3 5.1 %fusion.6 = f32[16,2,64,128]{3,2,1,0:T(8,128)S(1)} fusion(f32[16,2,128,64]{3,2,1,0:T(8,128)} %copy-done), kind=kOutput, calls=%fused_computation.11 | convolution fusion | flops 403144704 | bytes 2097152 | tf_op jit(solution)/shard_map/abkj,km->abjm/dot_general | solution.py:29
  12.3 0.7 fusion.17
  13.1 0.7 fusion.16
  13.9 0.0 copy-done.2
  13.9 0.8 fusion.10
  14.6 0.1 stack_reshape.7
  14.8 0.2 copy.29
  14.9 0.8 fusion.11
  15.7 0.1 stack_reshape.6
  15.9 0.2 copy.28
  16.0 3.2 %fusion.12 = bf16[16,8,2,2,256]{4,0,2,3,1:T(8,128)(2,1)S(1)} fusion(s32[8,256]{1,0:T(8,128)S(1)} %eq.20, f32[1,16,2,2048]{3,1,2,0:T(8,128)S(1)} %copy.29, f32[1,16,2,2048]{3,1,2,0:T(8,128)S(1)} %copy.28), kind=kOutput, calls=%fused_computation.18 | convolution fusion | flops 541589504 | bytes 794624 | tf_op jit(solution)/shard_map/cmro,ogs->mgrcs/dot_general | solution.py:79
  19.3 1.1 %broadcast_in_dim.15 = bf16[16,4,8,2,2,256]{5,0,4,3,2,1:T(8,128)(2,1)} broadcast(bf16[16,8,2,2,256]{4,0,3,2,1:T(8,128)(2,1)S(1)} %copy.30), dimensions={0,2,3,4,5} | broadcast | bytes 1310720 | tf_op jit(solution)/shard_map/broadcast_in_dim | solution.py:82
  20.4 7.3 %all-to-all-start = ((bf16[16,64,2,256]{3,0,2,1:T(8,128)(2,1)}), bf16[16,64,2,256]{3,0,2,1:T(8,128)(2,1)S(1)}, u32[]{:S(2)}, u32[]{:S(2)}) async-start(bf16[16,64,2,256]{3,0,2,1:T(8,128)(2,1)} %bitcast.18), calls=%async_computation | async-start | bytes 2097152 | tf_op jit(solution)/shard_map/all_to_all | solution.py:86
  27.7 0.1 dynamic_slice.3
  27.8 0.0 copy-start.1
  27.8 16.5 %copy.43 = bf16[64,384,256,1]{1,0,3,2:T(8,128)(2,1)} copy(bf16[64,384,256,1]{2,1,0,3:T(8,128)(2,1)} %bitcast.68) | data formatting | bytes 25165824 | tf_op args[1]
  44.3 0.0 copy-done.1
  44.4 0.1 broadcast_compare_fusion
  44.5 10.8 %all-to-all-done = bf16[16,64,2,256]{3,0,2,1:T(8,128)(2,1)S(1)} async-done(((bf16[16,64,2,256]{3,0,2,1:T(8,128)(2,1)}), bf16[16,64,2,256]{3,0,2,1:T(8,128)(2,1)S(1)}, u32[]{:S(2)}, u32[]{:S(2)}) %all-to-all-start) | async-done | bytes 1048608 | tf_op jit(solution)/shard_map/all_to_all | solution.py:86
  55.3 3.5 %copy.31 = bf16[16,64,2,256]{1,0,2,3:T(8,128)(2,1)S(1)} copy(bf16[16,64,2,256]{3,0,2,1:T(8,128)(2,1)S(1)} %all-to-all-done) | data formatting | bytes 2097152 | tf_op jit(solution)/shard_map/all_to_all | solution.py:86
  58.8 5.9 %convolution_bitcast_fusion = f32[16,2,384,256]{2,0,1,3:T(8,128)S(1)} fusion(bf16[16,64,2,256]{1,0,2,3:T(8,128)(2,1)S(1)} %copy.31, bf16[64,384,256,1]{1,0,3,2:T(8,128)(2,1)} %copy.43), kind=kOutput, calls=%fused_computation.9 | convolution fusion | flops 402653184 | bytes 26214400 | tf_op jit(solution)/shard_map/mrcs,rjs->mcjs/dot_general | solution.py:63
  64.7 5.4 %fusion.5 = (f32[16,384,256]{1,0,2:T(8,128)}, f32[16,384,256]{1,0,2:T(8,128)}) fusion(f32[16,2,384,256]{2,0,1,3:T(8,128)S(1)} %convolution_bitcast_fusion, pred[384,256]{0,1:T(8,128)(4,1)S(1)} %broadcast_compare_fusion), kind=kLoop, calls=%fused_computation.8 | loop fusion | flops 3145728 | bytes 25264128 | tf_op jit(solution)/shard_map/jit(_where)/select_n | solution.py:93
  70.1 6.6 %copy.34 = f32[16,384,256]{2,1,0:T(8,128)} copy(f32[16,384,256]{1,0,2:T(8,128)} %get-tuple-element.5) | data formatting | bytes 12582912 | tf_op jit(solution)/shard_map/jit(_where)/select_n | solution.py:93
  76.7 6.6 %copy.35 = f32[16,384,256]{2,1,0:T(8,128)} copy(f32[16,384,256]{1,0,2:T(8,128)} %get-tuple-element.6) | data formatting | bytes 12582912 | tf_op jit(solution)/shard_map/jit(_where)/select_n | solution.py:94
  83.3 20.6 %add_convert_fusion = bf16[8,16,2,384,256]{4,3,2,1,0:T(8,128)(2,1)} fusion(f32[8,2,384]{2,1,0:T(2,128)S(1)} %get-tuple-element.11, f32[16,384,256]{2,1,0:T(8,128)} %copy.35, f32[8,2,384]{2,1,0:T(2,128)S(1)} %get-tuple-element.10, f32[16,384,256]{2,1,0:T(8,128)} %copy.34), kind=kLoop, calls=%fused_computation | loop fusion | flops 100663296 | bytes 62963712 | tf_op jit(solution)/shard_map/convert_element_type | solution.py:99
  (5 shorter events, 0.1 us)
Async XLA Ops:
  2.4 1.3 %copy-start = (f32[16,2,128,64]{3,2,1,0:T(8,128)}, f32[16,2,128,64]{3,2,1,0:T(8,128)S(1)}, u32[]{:S(2)}) copy-start(f32[16,2,128,64]{3,2,1,0:T(8,128)S(1)} %reshape.86) | copy-start | bytes 3145732
  3.8 10.1 %copy-start.2 = (s32[2048]{0:T(1024)S(1)}, s32[2048]{0:T(1024)}, u32[]{:S(2)}) copy-start(s32[2048]{0:T(1024)} %param.6) | copy-start | bytes 24580
  20.4 34.9 %all-to-all-start = ((bf16[16,64,2,256]{3,0,2,1:T(8,128)(2,1)}), bf16[16,64,2,256]{3,0,2,1:T(8,128)(2,1)S(1)}, u32[]{:S(2)}, u32[]{:S(2)}) async-start(bf16[16,64,2,256]{3,0,2,1:T(8,128)(2,1)} %bitcast.18), calls=%async_computation | async-start | bytes 2097152 | tf_op jit(solution)/shard_map/all_to_all | solution.py:86
  27.8 16.5 %copy-start.1 = (f32[8,2,384]{2,1,0:T(2,128)S(1)}, f32[8,2,384]{2,1,0:T(2,128)}, u32[]{:S(2)}) copy-start(f32[8,2,384]{2,1,0:T(2,128)} %param.7) | copy-start | bytes 73732
where the time goes:
time: 105 us; the launch traced here: 104 us
  local copies, waits for them, and re-layouts  38.7 us (37%)
  other arithmetic  26.3 us (25%)
  matrix products  20.6 us (20%)
  waiting for transfers between devices  10.8 us (10%)
  starting transfers between devices  7.3 us (7%)
    convert_element_type x1, other arithmetic, local(): return (real_part * first + imag_part * second).astype(jnp.bfloat16)  20.6 us
    unnamed x7, local copies, waits for them, and re-layouts  17.8 us
    all_to_all x1, waiting for transfers between devices, local(): lax.all_to_all(copies, ('blk', 'order'), split_axis=1, concat_axis=1, til...  10.8 us
    all_to_all x1, starting transfers between devices, local(): lax.all_to_all(copies, ('blk', 'order'), split_axis=1, concat_axis=1, til...  7.3 us
    select_n x1, local copies, waits for them, and re-layouts, local(): real_part = jnp.where(live[None], harmonic[:, 0], 0.0)[None, :, None]  6.61 us
    select_n x1, local copies, waits for them, and re-layouts, local(): imag_part = jnp.where(live[None], harmonic[:, 1], 0.0)[None, :, None]  6.6 us
    dot_general x1, matrix products, add_cycles(): jnp.einsum('mrcs,rjs->mcjs', piece, table, preferred_element_type=jnp.flo...  5.86 us
    select_n x1, other arithmetic, local(): real_part = jnp.where(live[None], harmonic[:, 0], 0.0)[None, :, None]  5.4 us
  transfers between devices with their start and end apart: 1, of which 1 were waited for; matrix products, arithmetic and copies ran while one was open for 16% of the time, Pallas kernels for 0%

commit v1 on v0

--- a/solution.py
+++ b/solution.py
@@ -83,7 +83,15 @@
         by_owner[:, None], (maps_count, cycle_groups, groups, cycle_count, 2, slot_count)
     )
     copies = copies.reshape(maps_count, cycle_groups * groups * cycle_count, 2, slot_count)
-    every_cycle = lax.all_to_all(copies, ("blk", "order"), split_axis=1, concat_axis=1, tiled=True)
+    every_cycle = jnp.concatenate(
+        lax.all_to_all(
+            jnp.stack(jnp.split(copies, lax.axis_size(("blk", "order")), axis=1)),
+            ("blk", "order"),
+            0,
+            0,
+        ),
+        axis=1,
+    )
     harmonic = add_cycles(every_cycle, wigner_d)
     my_orders = lax.dynamic_slice_in_dim(
         order_of_slot, lax.axis_index("order") * slot_count, slot_count, 0

time: 105 us -> 123 us (1.17)
  local copies, waits for them, and re-layouts: 38.7 us -> 57.3 us
    unnamed x7 -> x38, local copies, waits for them, and re-layouts: 17.8 us -> 36.8 us
    all_to_all x1 -> x0, local copies, waits for them, and re-layouts: 3.54 us -> none  [local(): lax.all_to_all(copies, ('blk', 'order'), split_axis=1, concat_axis=1, til...]
    reshape x0 -> x1, local copies, waits for them, and re-layouts: none -> 3.54 us  [local(): jnp.concatenate(lax.all_to_all(jnp.stack(jnp.split(copies, lax.axis_size(...]
  transfers between devices with their start and end apart: 1 -> 1, of which waited for: 1 -> 1; matrix products, arithmetic and copies ran while one was open for 16% -> 14% of each run, Pallas kernels for 0% -> 0%
where the time goes in v1:
time: 123 us
  local copies, waits for them, and re-layouts  57.3 us (47%)
  other arithmetic  26.3 us (21%)
  matrix products  20.6 us (17%)
  waiting for transfers between devices  10.8 us (9%)
  starting transfers between devices  7.3 us (6%)
    unnamed x38, local copies, waits for them, and re-layouts  36.8 us
    convert_element_type x1, other arithmetic, local(): return (real_part * first + imag_part * second).astype(jnp.bfloat16)  20.6 us
    all_to_all x1, waiting for transfers between devices, local(): lax.all_to_all(jnp.stack(jnp.split(copies, lax.axis_size(('blk', 'order')...  10.8 us
    all_to_all x1, starting transfers between devices, local(): lax.all_to_all(jnp.stack(jnp.split(copies, lax.axis_size(('blk', 'order')...  7.3 us
    select_n x1, local copies, waits for them, and re-layouts, local(): real_part = jnp.where(live[None], harmonic[:, 0], 0.0)[None, :, None]  6.61 us
    select_n x1, local copies, waits for them, and re-layouts, local(): imag_part = jnp.where(live[None], harmonic[:, 1], 0.0)[None, :, None]  6.6 us
    dot_general x1, matrix products, add_cycles(): jnp.einsum('mrcs,rjs->mcjs', piece, table, preferred_element_type=jnp.flo...  5.86 us
    select_n x1, other arithmetic, local(): real_part = jnp.where(live[None], harmonic[:, 0], 0.0)[None, :, None]  5.4 us
  transfers between devices with their start and end apart: 1, of which 1 were waited for; matrix products, arithmetic and copies ran while one was open for 14% of the time, Pallas kernels for 0%

profile of v1, /device:TPU:0, one launch (start us, length us, event | category | flops | bytes accessed | tf_op | source)
XLA Modules:
  0.0 122.7 jit_solution(16169933105190356941)
XLA Ops:
  0.1 2.3 %reshape.94 = f32[16,2,128,64]{3,2,1,0:T(8,128)S(1)} reshape(f32[16,2,8192]{2,1,0:T(2,128)} %param.4) | data formatting | bytes 2097152 | tf_op jit(solution)/shard_map/reshape | solution.py:18
  2.5 1.3 %copy-done = f32[16,2,128,64]{3,2,1,0:T(8,128)} copy-done((f32[16,2,128,64]{3,2,1,0:T(8,128)}, f32[16,2,128,64]{3,2,1,0:T(8,128)S(1)}, u32[]{:S(2)}) %copy-start) | copy-done | bytes 1048600
  3.8 3.5 %convolution_bitcast_fusion.1 = f32[16,2,64,128]{3,2,1,0:T(8,128)S(1)} fusion(f32[16,2,128,64]{3,2,1,0:T(8,128)S(1)} %reshape.94), kind=kOutput, calls=%fused_computation.12 | convolution fusion | flops 402882560 | bytes 2097152 | tf_op jit(solution)/shard_map/abkj,km->abjm/dot_general | solution.py:28
  7.3 5.1 %fusion.6 = f32[16,2,64,128]{3,2,1,0:T(8,128)S(1)} fusion(f32[16,2,128,64]{3,2,1,0:T(8,128)} %copy-done), kind=kOutput, calls=%fused_computation.11 | convolution fusion | flops 403144704 | bytes 2097152 | tf_op jit(solution)/shard_map/abkj,km->abjm/dot_general | solution.py:29
  12.3 0.7 fusion.17
  13.1 0.7 fusion.16
  13.9 0.8 fusion.10
  14.9 0.8 fusion.11
  16.0 3.2 %fusion.12 = bf16[16,8,2,2,256]{4,0,2,3,1:T(8,128)(2,1)S(1)} fusion(s32[8,256]{1,0:T(8,128)S(1)} %eq.20, f32[1,16,2,2048]{3,1,2,0:T(8,128)S(1)} %copy.49, f32[1,16,2,2048]{3,1,2,0:T(8,128)S(1)} %copy.48), kind=kOutput, calls=%fused_computation.18 | convolution fusion | flops 541589504 | bytes 794624 | tf_op jit(solution)/shard_map/cmro,ogs->mgrcs/dot_general | solution.py:79
  19.4 0.6 constant_dynamic-update-slice_fusion.31
  20.0 0.6 constant_dynamic-update-slice_fusion.30
  20.6 0.6 constant_dynamic-update-slice_fusion.29
  21.2 0.6 constant_dynamic-update-slice_fusion.28
  21.9 0.6 constant_dynamic-update-slice_fusion.27
  22.5 0.6 constant_dynamic-update-slice_fusion.26
  23.1 0.6 constant_dynamic-update-slice_fusion.25
  23.7 0.6 constant_dynamic-update-slice_fusion.24
  24.3 0.6 constant_dynamic-update-slice_fusion.23
  24.9 0.6 constant_dynamic-update-slice_fusion.22
  25.5 0.6 constant_dynamic-update-slice_fusion.21
  26.1 0.6 constant_dynamic-update-slice_fusion.20
  26.8 0.6 constant_dynamic-update-slice_fusion.19
  27.4 0.6 constant_dynamic-update-slice_fusion.18
  28.0 0.6 constant_dynamic-update-slice_fusion.17
  28.6 0.6 constant_dynamic-update-slice_fusion.16
  30.4 0.6 constant_dynamic-update-slice_fusion.13
  31.1 0.6 constant_dynamic-update-slice_fusion.12
  31.7 0.6 constant_dynamic-update-slice_fusion.11
  32.3 0.6 constant_dynamic-update-slice_fusion.10
  32.9 0.6 constant_dynamic-update-slice_fusion.9
  33.5 0.6 constant_dynamic-update-slice_fusion.8
  34.1 0.6 constant_dynamic-update-slice_fusion.7
  34.7 0.6 constant_dynamic-update-slice_fusion.6
  35.3 0.6 constant_dynamic-update-slice_fusion.5
  36.0 0.6 constant_dynamic-update-slice_fusion.4
  36.6 0.6 constant_dynamic-update-slice_fusion.3
  37.2 0.6 constant_dynamic-update-slice_fusion.2
  37.8 0.6 constant_dynamic-update-slice_fusion.1
  38.4 0.6 constant_dynamic-update-slice_fusion
  39.0 7.3 %all-to-all-start = ((bf16[32,16,2,2,256]{4,1,3,2,0:T(8,128)(2,1)}), bf16[32,16,2,2,256]{4,1,3,2,0:T(8,128)(2,1)S(1)}, u32[]{:S(2)}, u32[]{:S(2)}) async-start(bf16[32,16,2,2,256]{4,1,3,2,0:T(8,128)(2,1)} %constant_dynamic-update-slice_fusion), calls=%async_computation | async-start | bytes 2097152 | tf_op jit(solution)/shard_map/all_to_all | solution.py:87
  46.4 16.5 %copy.63 = bf16[64,384,256,1]{1,0,3,2:T(8,128)(2,1)} copy(bf16[64,384,256,1]{2,1,0,3:T(8,128)(2,1)} %bitcast.199) | data formatting | bytes 25165824 | tf_op args[1]
  63.2 10.8 %all-to-all-done = bf16[32,16,2,2,256]{4,1,3,2,0:T(8,128)(2,1)S(1)} async-done(((bf16[32,16,2,2,256]{4,1,3,2,0:T(8,128)(2,1)}), bf16[32,16,2,2,256]{4,1,3,2,0:T(8,128)(2,1)S(1)}, u32[]{:S(2)}, u32[]{:S(2)}) %all-to-all-start) | async-done | bytes 1048608 | tf_op jit(solution)/shard_map/all_to_all | solution.py:87
  73.9 3.5 %copy.51 = bf16[16,64,2,256]{1,0,2,3:T(8,128)(2,1)S(1)} copy(bf16[16,64,2,256]{3,0,2,1:T(8,128)(2,1)S(1)} %bitcast.232) | data formatting | bytes 2097152 | tf_op jit(solution)/shard_map/reshape | solution.py:86
  77.5 5.9 %convolution_bitcast_fusion = f32[16,2,384,256]{2,0,1,3:T(8,128)S(1)} fusion(bf16[16,64,2,256]{1,0,2,3:T(8,128)(2,1)S(1)} %copy.51, bf16[64,384,256,1]{1,0,3,2:T(8,128)(2,1)} %copy.63), kind=kOutput, calls=%fused_computation.9 | convolution fusion | flops 402653184 | bytes 26214400 | tf_op jit(solution)/shard_map/mrcs,rjs->mcjs/dot_general | solution.py:63
  83.3 5.4 %fusion.5 = (f32[16,384,256]{1,0,2:T(8,128)}, f32[16,384,256]{1,0,2:T(8,128)}) fusion(f32[16,2,384,256]{2,0,1,3:T(8,128)S(1)} %convolution_bitcast_fusion, pred[384,256]{0,1:T(8,128)(4,1)S(1)} %broadcast_compare_fusion), kind=kLoop, calls=%fused_computation.8 | loop fusion | flops 3145728 | bytes 25264128 | tf_op jit(solution)/shard_map/jit(_where)/select_n | solution.py:101
  88.7 6.6 %copy.54 = f32[16,384,256]{2,1,0:T(8,128)} copy(f32[16,384,256]{1,0,2:T(8,128)} %get-tuple-element.5) | data formatting | bytes 12582912 | tf_op jit(solution)/shard_map/jit(_where)/select_n | solution.py:101
  95.4 6.6 %copy.55 = f32[16,384,256]{2,1,0:T(8,128)} copy(f32[16,384,256]{1,0,2:T(8,128)} %get-tuple-element.6) | data formatting | bytes 12582912 | tf_op jit(solution)/shard_map/jit(_where)/select_n | solution.py:102
  102.0 20.6 %add_convert_fusion = bf16[8,16,2,384,256]{4,3,2,1,0:T(8,128)(2,1)} fusion(f32[8,2,384]{2,1,0:T(2,128)S(1)} %get-tuple-element.11, f32[16,384,256]{2,1,0:T(8,128)} %copy.55, f32[8,2,384]{2,1,0:T(2,128)S(1)} %get-tuple-element.10, f32[16,384,256]{2,1,0:T(8,128)} %copy.54), kind=kLoop, calls=%fused_computation | loop fusion | flops 100663296 | bytes 62963712 | tf_op jit(solution)/shard_map/convert_element_type | solution.py:107
  (20 shorter events, 2.4 us)
Async XLA Ops:
  2.4 1.3 %copy-start = (f32[16,2,128,64]{3,2,1,0:T(8,128)}, f32[16,2,128,64]{3,2,1,0:T(8,128)S(1)}, u32[]{:S(2)}) copy-start(f32[16,2,128,64]{3,2,1,0:T(8,128)S(1)} %reshape.94) | copy-start | bytes 3145732
  3.8 10.1 %copy-start.2 = (s32[2048]{0:T(1024)S(1)}, s32[2048]{0:T(1024)}, u32[]{:S(2)}) copy-start(s32[2048]{0:T(1024)} %param.6) | copy-start | bytes 24580
  39.0 34.9 %all-to-all-start = ((bf16[32,16,2,2,256]{4,1,3,2,0:T(8,128)(2,1)}), bf16[32,16,2,2,256]{4,1,3,2,0:T(8,128)(2,1)S(1)}, u32[]{:S(2)}, u32[]{:S(2)}) async-start(bf16[32,16,2,2,256]{4,1,3,2,0:T(8,128)(2,1)} %constant_dynamic-update-slice_fusion), calls=%async_computation | async-start | bytes 2097152 | tf_op jit(solution)/shard_map/all_to_all | solution.py:87
  46.4 16.5 %copy-start.1 = (f32[8,2,384]{2,1,0:T(2,128)S(1)}, f32[8,2,384]{2,1,0:T(2,128)}, u32[]{:S(2)}) copy-start(f32[8,2,384]{2,1,0:T(2,128)} %param.7) | copy-start | bytes 73732
